TPU v7x, 32 devices: a whole 2x2x4 slice. The times are simulated.
32 devices in a mesh: rep: 2 (over x), zero: 16 (over z, y, core).
Axes of the slice: x: 2, y: 2, z: 4, core: 2. Of those that a mesh axis runs over, the one named last changes fastest.
Arguments:
- gated_input: bfloat16 [2, 2048, 4096], P('rep', 'zero'), may hold values from -6 to 6
- query_gate: bfloat16 [2, 2048, 4096], P('rep', 'zero'), may hold values from -12 to 12
- cotangent: bfloat16 [2, 2048, 4096], P('rep', 'zero'), may hold values from -8 to 8
- filters: float32 [2, 256, 128], P('rep', 'zero'), may hold values from -0.5 to 0.5
- first_moment: float32 [2, 256, 128], P('rep', 'zero'), may hold values from -0.03125 to 0.03125
- second_moment: float32 [2, 256, 128], P('rep', 'zero'), may hold values from 1e-06 to 0.0001
- step_index: int32 [1], replicated, may hold values from 0 to 999
Outputs:
- query_grad: bfloat16 [2, 2048, 4096], P('rep', 'zero')
- input_grad: bfloat16 [2, 2048, 4096], P('rep', 'zero')
- new_filters: float32 [2, 256, 128], P('rep', 'zero')
All inputs are finite; a program needn't handle non-finite values.
Results may differ from a plain program's by a relative error of at most 0.007.
Values may be sent and summed in bfloat16 or wider, within the bound.
No kernel may reach another device: no remote copies, remote signals or barrier semaphores. Data moves between devices by JAX's collectives and lax.ppermute only.
A program may use at most 256 MiB of HBM per device.

v0:
```python
from functools import partial
import jax
import jax.numpy as jnp
from jax import lax
from jax.sharding import PartitionSpec as P

CLIP_NORM = 1.0
BETA_ONE = 0.9
BETA_TWO = 0.95
LEARN_RATE = 0.05
ADAM_EPS = 1e-08


def swapped(value, axis, apart):
    mask = 2**apart
    pairs = [(source, source ^ mask) for source in range(lax.axis_size(axis))]
    return lax.ppermute(value, axis, pairs)


def passed_along(block, axis, distance):
    devices = range(lax.axis_size(axis))
    route = [(i - distance, i) for i in devices if i - distance in devices]
    return lax.ppermute(block, axis, route)


def circulant(half_filters):
    groups_all, filter_len = half_filters.shape
    flipped = half_filters[:, ::-1]
    doubled = jnp.concatenate([flipped, flipped], axis=1)
    tiled = jnp.tile(doubled, (1, filter_len))
    trimmed = tiled[:, : filter_len * (2 * filter_len - 1)]
    return trimmed.reshape(groups_all, filter_len, 2 * filter_len - 1)[:, :, filter_len - 1 :]


def blocked(rows_major, groups_all, filter_len):
    tok_rows, channels = rows_major.shape
    return rows_major.T.reshape(
        groups_all, channels // groups_all, tok_rows // filter_len, filter_len
    )


def unblocked(blocks):
    groups_all, group_width, block_count, filter_len = blocks.shape
    return blocks.reshape(groups_all * group_width, block_count * filter_len).T


def swap_bit(values, bit_number):
    return swapped(values, "rep", bit_number)


def on_device(gated_input, query_gate, cotangent, filters, first_moment, second_moment, step_index):
    inputs = gated_input[0]
    gate_values = query_gate[0]
    upstream = cotangent[0]
    tok_rows, channels = inputs.shape
    filter_len = filters.shape[2]
    shard_len = filters.shape[1]
    half_filters = lax.all_gather(filters[0].astype(jnp.bfloat16), "zero", axis=0, tiled=True)
    groups_all = half_filters.shape[0]
    circ_table = circulant(half_filters)
    index_row = lax.broadcasted_iota(jnp.int32, (filter_len, filter_len), 0)
    index_col = lax.broadcasted_iota(jnp.int32, (filter_len, filter_len), 1)
    lower_mask = (index_row >= index_col)[None]
    zero_half = jnp.zeros((), jnp.bfloat16)
    table_cur = jnp.where(lower_mask, circ_table, zero_half)
    table_prev = jnp.where(lower_mask, zero_half, circ_table)
    upstream_wide = upstream.astype(jnp.float32)
    mixed_rows = (upstream_wide * gate_values.astype(jnp.float32)).astype(jnp.bfloat16)
    tail_rows = passed_along(inputs, "zero", 1)
    head_rows = passed_along(mixed_rows, "zero", -1)
    input_ext = jnp.concatenate([tail_rows, inputs], axis=0)
    mixed_ext = jnp.concatenate([mixed_rows, head_rows], axis=0)
    input_blocks = blocked(input_ext, groups_all, filter_len)
    mixed_blocks = blocked(mixed_ext, groups_all, filter_len)
    input_cur = input_blocks[:, :, 1:]
    input_prev = input_blocks[:, :, :-1]
    mixed_own = mixed_blocks[:, :, :-1]
    mixed_next = mixed_blocks[:, :, 1:]
    conv_out = jnp.einsum(
        "gik,gcbk->gcbi", table_cur, input_cur, preferred_element_type=jnp.float32
    )
    conv_out = conv_out + jnp.einsum(
        "gik,gcbk->gcbi", table_prev, input_prev, preferred_element_type=jnp.float32
    )
    query_grad = (upstream_wide * unblocked(conv_out)).astype(jnp.bfloat16)
    back_blocks = jnp.einsum(
        "gki,gcbk->gcbi", table_cur, mixed_own, preferred_element_type=jnp.float32
    )
    back_blocks = back_blocks + jnp.einsum(
        "gki,gcbk->gcbi", table_prev, mixed_next, preferred_element_type=jnp.float32
    )
    input_grad = unblocked(back_blocks).astype(jnp.bfloat16)
    lag_cur = jnp.einsum("gcbi,gcbk->gik", mixed_own, input_cur, preferred_element_type=jnp.float32)
    lag_prev = jnp.einsum(
        "gcbi,gcbk->gik", mixed_own, input_prev, preferred_element_type=jnp.float32
    )
    square = filter_len * filter_len
    front_part = jnp.pad(
        jnp.where(lower_mask, lag_cur, 0.0).reshape(groups_all, square), ((0, 0), (filter_len, 0))
    )
    rear_part = jnp.pad(
        jnp.where(lower_mask, 0.0, lag_prev).reshape(groups_all, square), ((0, 0), (0, filter_len))
    )
    skewed = (front_part + rear_part).reshape(groups_all, filter_len, filter_len + 1).sum(axis=1)
    local_grad = skewed[:, 1:][:, ::-1]
    grad_full = lax.psum(local_grad.astype(jnp.bfloat16), "zero").astype(jnp.float32)
    total_sq = jnp.sum(grad_full * grad_full)
    grad_shard = lax.dynamic_slice_in_dim(
        grad_full, lax.axis_index("zero") * shard_len, shard_len, 0
    )
    clip_scale = jnp.minimum(1.0, CLIP_NORM / (jnp.sqrt(total_sq) + 1e-06))
    clipped = grad_shard * clip_scale
    step_count = step_index[0].astype(jnp.float32) + 1.0
    moment_one = BETA_ONE * first_moment[0] + (1.0 - BETA_ONE) * clipped
    moment_two = BETA_TWO * second_moment[0] + (1.0 - BETA_TWO) * clipped * clipped
    corrected_one = moment_one / (1.0 - jnp.power(BETA_ONE, step_count))
    corrected_two = moment_two / (1.0 - jnp.power(BETA_TWO, step_count))
    stepped = filters[0] - LEARN_RATE * corrected_one / (jnp.sqrt(corrected_two) + ADAM_EPS)
    bit_count = lax.axis_size("rep").bit_length() - 1
    partner_bit = step_index[0] % bit_count
    branches = [partial(swap_bit, bit_number=number) for number in range(bit_count)]
    partner_values = lax.switch(partner_bit, branches, stepped)
    new_filters = 0.5 * (stepped + partner_values)
    return (query_grad[None], input_grad[None], new_filters[None])


def solution(mesh):
    return jax.shard_map(
        on_device,
        mesh=mesh,
        in_specs=(
            P("rep", "zero", None),
            P("rep", "zero", None),
            P("rep", "zero", None),
            P("rep", "zero", None),
            P("rep", "zero", None),
            P("rep", "zero", None),
            P(),
        ),
        out_specs=(P("rep", "zero", None), P("rep", "zero", None), P("rep", "zero", None)),
        check_vma=False,
    )
```

profile of v0, /device:TPU:8, one launch (start us, length us, event | category | flops | bytes accessed | tf_op | source)
XLA Modules:
  0.0 408.8 jit_solution(13536019468429333070)
XLA Ops:
  7.2 1.9 collective-permute-start
  9.8 23.5 %all_gather.3 = bf16[256,128]{1,0:T(8,128)(2,1)S(1)} all-gather(bf16[16,128]{1,0:T(8,128)(2,1)S(1)} %bitcast_convert_fusion), channel_id=1, replica_groups=mesh['rep'=2,'zero'=16] {'zero'}, dimensions={0}, use_global_device_ids=true | all-gather | bytes 69632 | tf_op jit(solution)/shard_map/all_gather | solution.py:58
  34.8 41.7 %copy.70 = bf16[32,8,128,256]{3,1,2,0:T(8,128)(2,1)S(1)} copy(bf16[32,8,128,256]{3,2,1,0:T(8,128)(2,1)S(1)} %bitcast.64) | data formatting | bytes 33554432
  76.5 6.6 %slice.29 = bf16[256,32640]{1,0:T(8,128)(2,1)} slice(bf16[256,32768]{1,0:T(8,128)(2,1)S(1)} %bitcast.65), slice={[0:256], [0:32640]} | slice | bytes 33423360 | tf_op jit(solution)/shard_map/slice | solution.py:31
  83.1 56.8 %reshape.85 = bf16[256,128,255]{2,1,0:T(8,128)(2,1)} reshape(bf16[256,32640]{1,0:T(8,128)(2,1)} %slice.29) | data formatting | bytes 33423360 | tf_op jit(solution)/shard_map/reshape | solution.py:32
  140.0 1.4 maximum_bitcast_fusion
  141.4 2.5 copy.52
  143.9 2.5 reshape.83
  146.4 3.0 fusion.25
  149.4 9.6 %fusion.1 = f32[256,16,128]{2,1,0:T(8,128)S(1)} fusion(pred[128,128]{1,0:T(8,128)(4,1)S(1)} %iota_compare_fusion, bf16[256,128,255]{2,1,0:T(8,128)(2,1)} %reshape.85, bf16[256,16,1,128]{3,2,1,0:T(2,128)(2,1)S(1)} %get-tuple-element.12), kind=kOutput, calls=%fused_computation.6 | convolution fusion | flops 138412032 | bytes 11550720 | tf_op jit(solution)/shard_map/gik,gcbk->gcbi/dot_general | solution.py:79
  159.1 11.7 %fusion.10 = f32[256,16,128]{2,1,0:T(8,128)} fusion(f32[256,16,128]{2,1,0:T(8,128)S(1)} %fusion.1, pred[128,128]{1,0:T(8,128)(4,1)S(1)} %iota_compare_fusion, bf16[256,128,255]{2,1,0:T(8,128)(2,1)} %reshape.85, bf16[256,16,1,128]{3,2,1,0:T(2,128)(2,1)S(1)} %get-tuple-element.11), kind=kOutput, calls=%fused_computation.20 | convolution fusion | flops 138936320 | bytes 13647872 | tf_op jit(solution)/shard_map/gik,gcbk->gcbi/dot_general | solution.py:82
  170.8 2.1 copy.55
  172.9 3.0 fusion.9
  175.9 3.7 collective-permute-start.1
  180.3 11.6 %collective-permute-done.1 = bf16[128,4096]{1,0:T(8,128)(2,1)} collective-permute-done((bf16[128,4096]{1,0:T(8,128)(2,1)S(1)}, bf16[128,4096]{1,0:T(8,128)(2,1)}, u32[]{:S(2)}, u32[]{:S(2)}) %collective-permute-start.1) | collective-permute-done | bytes 1048608 | tf_op jit(solution)/shard_map/ppermute | solution.py:23
  191.9 1.4 maximum_bitcast_fusion.1
  193.3 2.5 copy.56
  195.8 2.5 reshape.88
  198.3 3.8 fusion.24
  202.1 7.2 %convolution_select_fusion = f32[256,128,128]{2,1,0:T(8,128)} fusion(pred[128,128]{1,0:T(8,128)(4,1)S(1)} %iota_compare_fusion, bf16[256,16,1,128]{3,2,1,0:T(2,128)(2,1)S(1)} %copy-done.5, bf16[256,16,1,128]{3,2,1,0:T(2,128)(2,1)S(1)} %get-tuple-element.10), kind=kOutput, calls=%fused_computation.1 | convolution fusion | flops 138412032 | bytes 18890752 | tf_op jit(solution)/shard_map/gcbi,gcbk->gik/dot_general | solution.py:94
  209.3 7.1 %convolution_select_fusion.1 = f32[256,128,128]{2,1,0:T(8,128)} fusion(pred[128,128]{1,0:T(8,128)(4,1)S(1)} %iota_compare_fusion, bf16[256,16,1,128]{3,2,1,0:T(2,128)(2,1)S(1)} %copy-done.3, bf16[256,16,1,128]{3,2,1,0:T(2,128)(2,1)S(1)} %get-tuple-element.10), kind=kOutput, calls=%fused_computation.2 | convolution fusion | flops 138412032 | bytes 18890752 | tf_op jit(solution)/shard_map/gcbi,gcbk->gik/dot_general | solution.py:93
  216.4 17.7 %copy.64 = f32[256,128,128]{0,2,1:T(8,128)} copy(f32[256,128,128]{2,1,0:T(8,128)} %convolution_select_fusion) | data formatting | bytes 33554432 | tf_op jit(solution)/shard_map/reshape | solution.py:102
  234.1 17.7 %copy.63 = f32[256,128,128]{0,2,1:T(8,128)} copy(f32[256,128,128]{2,1,0:T(8,128)} %convolution_select_fusion.1) | data formatting | bytes 33554432 | tf_op jit(solution)/shard_map/reshape | solution.py:99
  251.9 18.0 %pad_add_fusion = f32[256,16512]{0,1:T(8,128)} fusion(f32[256,16384]{0,1:T(8,128)} %bitcast.62, f32[256,16384]{0,1:T(8,128)} %bitcast.63), kind=kLoop, calls=%fused_computation | loop fusion | flops 4227072 | bytes 50462720 | tf_op jit(solution)/shard_map/add | solution.py:104
  269.9 18.0 %reshape.93 = f32[256,128,129]{0,2,1:T(8,128)} reshape(f32[256,16512]{0,1:T(8,128)} %pad_add_fusion) | data formatting | bytes 33816576 | tf_op jit(solution)/shard_map/reshape | solution.py:104
  287.9 7.3 %reduce_sum.18 = bf16[256,129]{0,1:T(8,128)(2,1)S(1)} reduce(f32[256,128,129]{0,2,1:T(8,128)} %reshape.93, f32[]{:T(128)} %constant.9.clone.1), dimensions={1}, to_apply=%region_0.1 | reduce | flops 4194048 | bytes 16974340 | tf_op jit(solution)/shard_map/reduce_sum | solution.py:104
  296.2 10.4 %fusion = f32[256,16,128]{2,1,0:T(8,128)} fusion(pred[128,128]{1,0:T(8,128)(4,1)S(1)} %iota_compare_fusion, bf16[256,128,255]{2,1,0:T(8,128)(2,1)} %reshape.85, bf16[256,16,1,128]{3,2,1,0:T(2,128)(2,1)S(1)} %copy-done.1), kind=kOutput, calls=%fused_computation.5 | convolution fusion | flops 138412032 | bytes 11550720 | tf_op jit(solution)/shard_map/gki,gcbk->gcbi/dot_general | solution.py:86
  306.5 78.4 %all-reduce.4.cloned.1.call-done = bf16[256,128]{1,0:T(8,128)(2,1)} async-done(((bf16[256,128]{1,0:T(8,128)(2,1)}), bf16[256,128]{1,0:T(8,128)(2,1)}) %all-reduce.4.cloned.1.call-update) | async-done | bytes 65552 | tf_op jit(solution)/shard_map/psum | solution.py:106
  385.0 1.5 multiply_reduce_fusion
  388.1 1.5 collective-permute-start.2
  389.6 10.4 %add_convert_fusion = bf16[256,16,128]{2,1,0:T(8,128)(2,1)S(1)} fusion(f32[256,16,128]{2,1,0:T(8,128)} %fusion, pred[128,128]{1,0:T(8,128)(4,1)S(1)} %iota_compare_fusion, bf16[256,128,255]{2,1,0:T(8,128)(2,1)} %reshape.85, bf16[256,16,1,128]{3,2,1,0:T(2,128)(2,1)} %get-tuple-element.9), kind=kOutput, calls=%fused_computation.19 | convolution fusion | flops 139460608 | bytes 13647872 | tf_op jit(solution)/shard_map/gki,gcbk->gcbi/dot_general | solution.py:89
  400.0 1.3 copy.59
  (35 shorter events, 4.7 us)
Async XLA Ops:
  7.2 377.8 %all-reduce.4.cloned.1.call-start = ((), (), s32[]{:S(2)}) async-start(), calls=%async_computation | async-start | bytes 131072 | tf_op jit(solution)/shard_map/psum | solution.py:106
  7.2 132.8 %collective-permute-start = (bf16[128,4096]{1,0:T(8,128)(2,1)}, bf16[128,4096]{1,0:T(8,128)(2,1)}, u32[]{:S(2)}, u32[]{:S(2)}) collective-permute-start(bf16[128,4096]{1,0:T(8,128)(2,1)} %bitcast.69), channel_id=1, source_target_pairs={{0,1},{1,2},{2,3},{3,4},{4,5},{5,6},{6,7},{7,8},{8,9},{9,10},{10,1... | collective-permute-start | bytes 3145736 | tf_op jit(solution)/shard_map/ppermute | solution.py:23
  83.1 56.8 %copy-start.6 = (bf16[1,128,4096]{2,1,0:T(8,128)(2,1)S(1)}, bf16[1,128,4096]{2,1,0:T(8,128)(2,1)}, u32[]{:S(2)}) copy-start(bf16[1,128,4096]{2,1,0:T(8,128)(2,1)} %param.7) | copy-start | bytes 3145732
  149.4 9.7 %copy-start.2 = (bf16[256,16,1,128]{3,2,1,0:T(2,128)(2,1)}, bf16[256,16,1,128]{3,2,1,0:T(2,128)(2,1)S(1)}, u32[]{:S(2)}) copy-start(bf16[256,16,1,128]{3,2,1,0:T(2,128)(2,1)S(1)} %get-tuple-element.12) | copy-start | bytes 3145732
  149.4 9.7 %copy-start.4 = (bf16[256,16,1,128]{3,2,1,0:T(2,128)(2,1)}, bf16[256,16,1,128]{3,2,1,0:T(2,128)(2,1)S(1)}, u32[]{:S(2)}) copy-start(bf16[256,16,1,128]{3,2,1,0:T(2,128)(2,1)S(1)} %get-tuple-element.11) | copy-start | bytes 3145732
  175.9 16.0 %collective-permute-start.1 = (bf16[128,4096]{1,0:T(8,128)(2,1)S(1)}, bf16[128,4096]{1,0:T(8,128)(2,1)}, u32[]{:S(2)}, u32[]{:S(2)}) collective-permute-start(bf16[128,4096]{1,0:T(8,128)(2,1)S(1)} %get-tuple-element.13), channel_id=1, source_target_pairs={{1,0},{2,1},{3,2},{4,3},{5,4},{6,5},{7,6},{8,7},{9,8},{10,9},{11,1... | collective-permute-start | bytes 3145736 | tf_op jit(solution)/shard_map/ppermute | solution.py:23
  198.3 3.8 copy-start.5
  202.1 7.2 %copy-start = (bf16[256,16,1,128]{3,2,1,0:T(2,128)(2,1)}, bf16[256,16,1,128]{3,2,1,0:T(2,128)(2,1)S(1)}, u32[]{:S(2)}) copy-start(bf16[256,16,1,128]{3,2,1,0:T(2,128)(2,1)S(1)} %get-tuple-element.10) | copy-start | bytes 3145732
  202.1 7.2 %copy-start.3 = (bf16[256,16,1,128]{3,2,1,0:T(2,128)(2,1)S(1)}, bf16[256,16,1,128]{3,2,1,0:T(2,128)(2,1)}, u32[]{:S(2)}) copy-start(bf16[256,16,1,128]{3,2,1,0:T(2,128)(2,1)} %copy-done.2) | copy-start | bytes 3145732
  287.9 8.3 %copy-start.1 = (bf16[256,16,1,128]{3,2,1,0:T(2,128)(2,1)S(1)}, bf16[256,16,1,128]{3,2,1,0:T(2,128)(2,1)}, u32[]{:S(2)}) copy-start(bf16[256,16,1,128]{3,2,1,0:T(2,128)(2,1)} %copy-done) | copy-start | bytes 3145732
  296.1 91.9 %copy-start.7 = (f32[1,16,128]{2,1,0:T(8,128)S(1)}, f32[1,16,128]{2,1,0:T(8,128)}, u32[]{:S(2)}) copy-start(f32[1,16,128]{2,1,0:T(8,128)} %param.10) | copy-start | bytes 24580
  296.2 91.9 %copy-start.8 = (f32[1,16,128]{2,1,0:T(8,128)S(1)}, f32[1,16,128]{2,1,0:T(8,128)}, u32[]{:S(2)}) copy-start(f32[1,16,128]{2,1,0:T(8,128)} %param.12) | copy-start | bytes 24580
  296.2 91.9 %copy-start.9 = (f32[1,16,128]{2,1,0:T(8,128)S(1)}, f32[1,16,128]{2,1,0:T(8,128)}, u32[]{:S(2)}) copy-start(f32[1,16,128]{2,1,0:T(8,128)} %param.11) | copy-start | bytes 24580
  388.1 13.2 %collective-permute-start.2 = (f32[16,128]{1,0:T(8,128)S(1)}, f32[16,128]{1,0:T(8,128)S(1)}, u32[]{:S(2)}, u32[]{:S(2)}) collective-permute-start(f32[16,128]{1,0:T(8,128)S(1)} %fusion.17), channel_id=1, source_target_pairs={{0,16},{16,0},{1,17},{17,1},{2,18},{18,2},{3,19},{19,3},{4,20},{20... | collective-permute-start | bytes 24584 | tf_op jit(solution)/shard_map/ppermute | solution.py:17
Sparse Core Ops, SparseCore 0:
  296.3 88.6 all-reduce.3
where the time goes:
time: 410 us; the launch traced here: 409 us
  local copies, waits for them, and re-layouts  181 us (44%)
  waiting for transfers between devices  90 us (22%)
  matrix products  56.3 us (14%)
  other arithmetic  34.8 us (8%)
  blocking collectives  23.5 us (6%)
  between operations  15.7 us (4%)
  starting transfers between devices  7.19 us (2%)
    psum x1, waiting for transfers between devices, on_device(): lax.psum(local_grad.astype(jnp.bfloat16), 'zero').astype(jnp.float32)  78.4 us
    reshape x1, local copies, waits for them, and re-layouts, circulant(): trimmed.reshape(groups_all, filter_len, 2 * filter_len - 1)  56.8 us
    unnamed x22, local copies, waits for them, and re-layouts  41.9 us
    all_gather x1, blocking collectives, on_device(): lax.all_gather(filters[0].astype(jnp.bfloat16), 'zero', axis=0, tiled=True)  23.5 us
    add x1, other arithmetic, on_device(): front_part + rear_part  18 us
    reshape x1, local copies, waits for them, and re-layouts, on_device(): (front_part + rear_part).reshape(groups_all, filter_len, filter_len + 1)  18 us
    reshape x1, local copies, waits for them, and re-layouts, on_device(): jnp.where(lower_mask, 0.0, lag_prev).reshape(groups_all, square)  17.7 us
    reshape x1, local copies, waits for them, and re-layouts, on_device(): jnp.where(lower_mask, lag_cur, 0.0).reshape(groups_all, square)  17.7 us
  transfers between devices with their start and end apart: 4, of which 2 were waited for; matrix products, arithmetic and copies ran while one was open for 32% of the time, Pallas kernels for 0%

commit v1 on v0

--- a/solution.py
+++ b/solution.py
@@ -55,7 +55,23 @@
     tok_rows, channels = inputs.shape
     filter_len = filters.shape[2]
     shard_len = filters.shape[1]
-    half_filters = lax.all_gather(filters[0].astype(jnp.bfloat16), "zero", axis=0, tiled=True)
+    x = filters[0].astype(jnp.bfloat16)
+    size, mine, extent = (lax.axis_size("zero"), lax.axis_index("zero"), x.shape[0])
+    right = [(i_2, (i_2 + 1) % size) for i_2 in range(size)]
+    backward = [(i_2, (i_2 - 1) % size) for i_2 in range(size)]
+    out = jnp.zeros((*x.shape[:0], size * extent, *x.shape[0 + 1 :]), x.dtype)
+    out = lax.dynamic_update_slice_in_dim(out, x, mine * extent, axis=0)
+    from_left = from_right = x
+    half = size // 2
+    for turn in range(1, half + 1):
+        from_left = lax.ppermute(from_left, "zero", right)
+        out = lax.dynamic_update_slice_in_dim(out, from_left, (mine - turn) % size * extent, axis=0)
+        if turn < size - half:
+            from_right = lax.ppermute(from_right, "zero", backward)
+            out = lax.dynamic_update_slice_in_dim(
+                out, from_right, (mine + turn) % size * extent, axis=0
+            )
+    half_filters = out
     groups_all = half_filters.shape[0]
     circ_table = circulant(half_filters)
     index_row = lax.broadcasted_iota(jnp.int32, (filter_len, filter_len), 0)

time: 410 us -> 427 us (1.041)
  waiting for transfers between devices: 90 us -> 114 us
  blocking collectives: 23.5 us -> 0 us
  starting transfers between devices: 7.19 us -> 23.9 us
    all_gather x1 -> x0, blocking collectives: 23.5 us -> none  [on_device(): lax.all_gather(filters[0].astype(jnp.bfloat16), 'zero', axis=0, tiled=True)]
    ppermute x0 -> x15, waiting for transfers between devices: none -> 22.8 us  [the longest x8 22.6 us: on_device(): from_left = lax.ppermute(from_left, 'zero', right)]
    ppermute x0 -> x15, starting transfers between devices: none -> 18.5 us  [the longest x7 17.7 us: on_device(): from_right = lax.ppermute(from_right, 'zero', backward)]
    unnamed x22 -> x24, local copies, waits for them, and re-layouts: 41.9 us -> 41.9 us
  transfers between devices with their start and end apart: 4 -> 19, of which waited for: 2 -> 9; matrix products, arithmetic and copies ran while one was open for 32% -> 30% of each run, Pallas kernels for 0% -> 0%
where the time goes in v1:
time: 427 us; the launch traced here: 425 us
  local copies, waits for them, and re-layouts  182 us (43%)
  waiting for transfers between devices  114 us (27%)
  matrix products  56.2 us (13%)
  other arithmetic  33.1 us (8%)
  starting transfers between devices  23.9 us (6%)
  between operations  16 us (4%)
    psum x1, waiting for transfers between devices, on_device(): lax.psum(local_grad.astype(jnp.bfloat16), 'zero').astype(jnp.float32)  80 us
    reshape x1, local copies, waits for them, and re-layouts, circulant(): trimmed.reshape(groups_all, filter_len, 2 * filter_len - 1)  56.8 us
    unnamed x24, local copies, waits for them, and re-layouts  41.9 us
    ppermute x8, waiting for transfers between devices, on_device(): from_left = lax.ppermute(from_left, 'zero', right)  22.6 us
    reshape x1, local copies, waits for them, and re-layouts, on_device(): (front_part + rear_part).reshape(groups_all, filter_len, filter_len + 1)  18 us
    add x1, other arithmetic, on_device(): front_part + rear_part  18 us
    reshape x1, local copies, waits for them, and re-layouts, on_device(): jnp.where(lower_mask, 0.0, lag_prev).reshape(groups_all, square)  17.8 us
    reshape x1, local copies, waits for them, and re-layouts, on_device(): jnp.where(lower_mask, lag_cur, 0.0).reshape(groups_all, square)  17.8 us
  transfers between devices with their start and end apart: 19, of which 9 were waited for; matrix products, arithmetic and copies ran while one was open for 30% of the time, Pallas kernels for 0%

profile of v1, /device:TPU:8, one launch (start us, length us, event | category | flops | bytes accessed | tf_op | source)
XLA Modules:
  0.0 425.4 jit_solution(3636167298958555643)
XLA Ops:
  7.9 2.6 collective-permute-start.2
  15.6 12.4 %collective-permute-done.3 = bf16[16,128]{1,0:T(8,128)(2,1)S(1)} collective-permute-done((bf16[16,128]{1,0:T(8,128)(2,1)S(1)}, bf16[16,128]{1,0:T(8,128)(2,1)S(1)}, u32[]{:S(2)}, u32[]{:S(2)}) %collective-permute-start.3) | collective-permute-done | bytes 4128 | tf_op jit(solution)/shard_map/ppermute | solution.py:67
  28.0 2.6 collective-permute-start.6
  31.9 2.6 collective-permute-start.8
  35.9 2.6 collective-permute-start.10
  39.8 2.6 collective-permute-start.12
  43.7 2.6 collective-permute-start.14
  47.7 3.9 collective-permute-done.15
  53.1 41.7 %copy.70 = bf16[32,8,128,256]{3,1,2,0:T(8,128)(2,1)S(1)} copy(bf16[32,8,128,256]{3,2,1,0:T(8,128)(2,1)S(1)} %bitcast.65) | data formatting | bytes 33554432
  94.8 6.8 %slice.29 = bf16[256,32640]{1,0:T(8,128)(2,1)} slice(bf16[256,32768]{1,0:T(8,128)(2,1)S(1)} %bitcast.66), slice={[0:256], [0:32640]} | slice | bytes 33423360 | tf_op jit(solution)/shard_map/slice | solution.py:31
  101.5 56.8 %reshape.85 = bf16[256,128,255]{2,1,0:T(8,128)(2,1)} reshape(bf16[256,32640]{1,0:T(8,128)(2,1)} %slice.29) | data formatting | bytes 33423360 | tf_op jit(solution)/shard_map/reshape | solution.py:32
  159.8 2.5 copy.52
  162.2 2.5 reshape.83
  164.8 3.0 fusion.25
  167.8 9.6 %fusion.1 = f32[256,16,128]{2,1,0:T(8,128)S(1)} fusion(pred[128,128]{1,0:T(8,128)(4,1)S(1)} %iota_compare_fusion, bf16[256,128,255]{2,1,0:T(8,128)(2,1)} %reshape.85, bf16[256,16,1,128]{3,2,1,0:T(2,128)(2,1)S(1)} %get-tuple-element.11), kind=kOutput, calls=%fused_computation.6 | convolution fusion | flops 138412032 | bytes 11550720 | tf_op jit(solution)/shard_map/gik,gcbk->gcbi/dot_general | solution.py:95
  177.4 11.7 %fusion.10 = f32[256,16,128]{2,1,0:T(8,128)} fusion(f32[256,16,128]{2,1,0:T(8,128)S(1)} %fusion.1, pred[128,128]{1,0:T(8,128)(4,1)S(1)} %iota_compare_fusion, bf16[256,128,255]{2,1,0:T(8,128)(2,1)} %reshape.85, bf16[256,16,1,128]{3,2,1,0:T(2,128)(2,1)S(1)} %get-tuple-element.10), kind=kOutput, calls=%fused_computation.20 | convolution fusion | flops 138936320 | bytes 13647872 | tf_op jit(solution)/shard_map/gik,gcbk->gcbi/dot_general | solution.py:98
  189.1 2.2 copy.55
  191.3 2.6 fusion.9
  196.6 11.6 %collective-permute-done.16 = bf16[128,4096]{1,0:T(8,128)(2,1)S(1)} collective-permute-done((bf16[128,4096]{1,0:T(8,128)(2,1)S(1)}, bf16[128,4096]{1,0:T(8,128)(2,1)S(1)}, u32[]{:S(2)}, u32[]{:S(2)}) %collective-permute-start.16) | collective-permute-done | bytes 1048608 | tf_op jit(solution)/shard_map/ppermute | solution.py:23
  208.3 2.5 copy.56
  210.7 2.5 reshape.88
  213.3 3.8 fusion.24
  217.1 7.2 %convolution_select_fusion = f32[256,128,128]{2,1,0:T(8,128)} fusion(pred[128,128]{1,0:T(8,128)(4,1)S(1)} %iota_compare_fusion, bf16[256,16,1,128]{3,2,1,0:T(2,128)(2,1)S(1)} %copy-done.5, bf16[256,16,1,128]{3,2,1,0:T(2,128)(2,1)S(1)} %get-tuple-element.9), kind=kOutput, calls=%fused_computation.1 | convolution fusion | flops 138412032 | bytes 18890752 | tf_op jit(solution)/shard_map/gcbi,gcbk->gik/dot_general | solution.py:110
  224.3 7.1 %convolution_select_fusion.1 = f32[256,128,128]{2,1,0:T(8,128)} fusion(pred[128,128]{1,0:T(8,128)(4,1)S(1)} %iota_compare_fusion, bf16[256,16,1,128]{3,2,1,0:T(2,128)(2,1)S(1)} %copy-done.3, bf16[256,16,1,128]{3,2,1,0:T(2,128)(2,1)S(1)} %get-tuple-element.9), kind=kOutput, calls=%fused_computation.2 | convolution fusion | flops 138412032 | bytes 18890752 | tf_op jit(solution)/shard_map/gcbi,gcbk->gik/dot_general | solution.py:109
  231.4 17.8 %copy.64 = f32[256,128,128]{0,2,1:T(8,128)} copy(f32[256,128,128]{2,1,0:T(8,128)} %convolution_select_fusion) | data formatting | bytes 33554432 | tf_op jit(solution)/shard_map/reshape | solution.py:118
  249.1 17.8 %copy.63 = f32[256,128,128]{0,2,1:T(8,128)} copy(f32[256,128,128]{2,1,0:T(8,128)} %convolution_select_fusion.1) | data formatting | bytes 33554432 | tf_op jit(solution)/shard_map/reshape | solution.py:115
  266.9 18.0 %pad_add_fusion = f32[256,16512]{0,1:T(8,128)} fusion(f32[256,16384]{0,1:T(8,128)} %bitcast.63, f32[256,16384]{0,1:T(8,128)} %bitcast.64), kind=kLoop, calls=%fused_computation | loop fusion | flops 4227072 | bytes 50462720 | tf_op jit(solution)/shard_map/add | solution.py:120
  284.9 18.0 %reshape.93 = f32[256,128,129]{0,2,1:T(8,128)} reshape(f32[256,16512]{0,1:T(8,128)} %pad_add_fusion) | data formatting | bytes 33816576 | tf_op jit(solution)/shard_map/reshape | solution.py:120
  302.9 7.3 %reduce_sum.18 = bf16[256,129]{0,1:T(8,128)(2,1)S(1)} reduce(f32[256,128,129]{0,2,1:T(8,128)} %reshape.93, f32[]{:T(128)} %constant.128.clone.1), dimensions={1}, to_apply=%region_0.1 | reduce | flops 4194048 | bytes 16974340 | tf_op jit(solution)/shard_map/reduce_sum | solution.py:120
  311.2 10.3 %fusion = f32[256,16,128]{2,1,0:T(8,128)} fusion(pred[128,128]{1,0:T(8,128)(4,1)S(1)} %iota_compare_fusion, bf16[256,128,255]{2,1,0:T(8,128)(2,1)} %reshape.85, bf16[256,16,1,128]{3,2,1,0:T(2,128)(2,1)S(1)} %copy-done.1), kind=kOutput, calls=%fused_computation.5 | convolution fusion | flops 138412032 | bytes 11550720 | tf_op jit(solution)/shard_map/gki,gcbk->gcbi/dot_general | solution.py:102
  321.5 80.0 %all-reduce.4.cloned.1.call-done = bf16[256,128]{1,0:T(8,128)(2,1)} async-done(((bf16[256,128]{1,0:T(8,128)(2,1)}), bf16[256,128]{1,0:T(8,128)(2,1)}) %all-reduce.4.cloned.1.call-update) | async-done | bytes 65552 | tf_op jit(solution)/shard_map/psum | solution.py:122
  406.2 10.4 %add_convert_fusion = bf16[256,16,128]{2,1,0:T(8,128)(2,1)S(1)} fusion(f32[256,16,128]{2,1,0:T(8,128)} %fusion, pred[128,128]{1,0:T(8,128)(4,1)S(1)} %iota_compare_fusion, bf16[256,128,255]{2,1,0:T(8,128)(2,1)} %reshape.85, bf16[256,16,1,128]{3,2,1,0:T(2,128)(2,1)} %get-tuple-element.8), kind=kOutput, calls=%fused_computation.19 | convolution fusion | flops 139460608 | bytes 13647872 | tf_op jit(solution)/shard_map/gki,gcbk->gcbi/dot_general | solution.py:105
  (82 shorter events, 23.9 us)
Async XLA Ops:
  7.2 394.4 %all-reduce.4.cloned.1.call-start = ((), (), s32[]{:S(2)}) async-start(), calls=%async_computation | async-start | bytes 131072 | tf_op jit(solution)/shard_map/psum | solution.py:122
  7.9 4.9 %collective-permute-start.1 = (bf16[16,128]{1,0:T(8,128)(2,1)S(1)}, bf16[16,128]{1,0:T(8,128)(2,1)S(1)}, u32[]{:S(2)}, u32[]{:S(2)}) collective-permute-start(bf16[16,128]{1,0:T(8,128)(2,1)S(1)} %get-tuple-element.7), channel_id=1, source_target_pairs={{0,1},{1,2},{2,3},{3,4},{4,5},{5,6},{6,7},{7,8},{8,9},{9,10},{10,1... | collective-permute-start | bytes 12296 | tf_op jit(solution)/shard_map/ppermute | solution.py:67
  7.9 5.6 %collective-permute-start.2 = (bf16[16,128]{1,0:T(8,128)(2,1)S(1)}, bf16[16,128]{1,0:T(8,128)(2,1)S(1)}, u32[]{:S(2)}, u32[]{:S(2)}) collective-permute-start(bf16[16,128]{1,0:T(8,128)(2,1)S(1)} %get-tuple-element.7), channel_id=1, source_target_pairs={{0,15},{1,0},{2,1},{3,2},{4,3},{5,4},{6,5},{7,6},{8,7},{9,8},{10,9... | collective-permute-start | bytes 12296 | tf_op jit(solution)/shard_map/ppermute | solution.py:70
  10.6 147.8 %collective-permute-start = (bf16[128,4096]{1,0:T(8,128)(2,1)}, bf16[128,4096]{1,0:T(8,128)(2,1)}, u32[]{:S(2)}, u32[]{:S(2)}) collective-permute-start(bf16[128,4096]{1,0:T(8,128)(2,1)} %bitcast.70), channel_id=1, source_target_pairs={{0,1},{1,2},{2,3},{3,4},{4,5},{5,6},{6,7},{7,8},{8,9},{9,10},{10,1... | collective-permute-start | bytes 3145736 | tf_op jit(solution)/shard_map/ppermute | solution.py:23
  12.8 15.1 %collective-permute-start.3 = (bf16[16,128]{1,0:T(8,128)(2,1)S(1)}, bf16[16,128]{1,0:T(8,128)(2,1)S(1)}, u32[]{:S(2)}, u32[]{:S(2)}) collective-permute-start(bf16[16,128]{1,0:T(8,128)(2,1)S(1)} %collective-permute-done.1), channel_id=1, source_target_pairs={{0,1},{1,2},{2,3},{3,4},{4,5},{5,6},{6,7},{7,8},{8,9},{9,10},{10,1... | collective-permute-start | bytes 12296 | tf_op jit(solution)/shard_map/ppermute | solution.py:67
  13.6 14.4 %collective-permute-start.4 = (bf16[16,128]{1,0:T(8,128)(2,1)S(1)}, bf16[16,128]{1,0:T(8,128)(2,1)S(1)}, u32[]{:S(2)}, u32[]{:S(2)}) collective-permute-start(bf16[16,128]{1,0:T(8,128)(2,1)S(1)} %collective-permute-done.2), channel_id=1, source_target_pairs={{0,15},{1,0},{2,1},{3,2},{4,3},{5,4},{6,5},{7,6},{8,7},{9,8},{10,9... | collective-permute-start | bytes 12296 | tf_op jit(solution)/shard_map/ppermute | solution.py:70
  28.0 3.9 collective-permute-start.5
  28.0 4.0 collective-permute-start.6
  31.9 3.9 collective-permute-start.7
  31.9 3.9 collective-permute-start.8
  35.8 3.9 collective-permute-start.9
  35.9 3.9 collective-permute-start.10
  39.8 3.9 collective-permute-start.11
  39.8 3.9 collective-permute-start.12
  43.7 3.9 collective-permute-start.13
  43.7 3.9 collective-permute-start.14
  47.6 3.9 collective-permute-start.15
  101.5 56.8 %copy-start.6 = (bf16[1,128,4096]{2,1,0:T(8,128)(2,1)S(1)}, bf16[1,128,4096]{2,1,0:T(8,128)(2,1)}, u32[]{:S(2)}) copy-start(bf16[1,128,4096]{2,1,0:T(8,128)(2,1)} %param.7) | copy-start | bytes 3145732
  167.8 9.7 %copy-start.2 = (bf16[256,16,1,128]{3,2,1,0:T(2,128)(2,1)}, bf16[256,16,1,128]{3,2,1,0:T(2,128)(2,1)S(1)}, u32[]{:S(2)}) copy-start(bf16[256,16,1,128]{3,2,1,0:T(2,128)(2,1)S(1)} %get-tuple-element.11) | copy-start | bytes 3145732
  167.8 9.7 %copy-start.4 = (bf16[256,16,1,128]{3,2,1,0:T(2,128)(2,1)}, bf16[256,16,1,128]{3,2,1,0:T(2,128)(2,1)S(1)}, u32[]{:S(2)}) copy-start(bf16[256,16,1,128]{3,2,1,0:T(2,128)(2,1)S(1)} %get-tuple-element.10) | copy-start | bytes 3145732
  189.1 2.2 copy-start.7
  193.9 14.2 %collective-permute-start.16 = (bf16[128,4096]{1,0:T(8,128)(2,1)S(1)}, bf16[128,4096]{1,0:T(8,128)(2,1)S(1)}, u32[]{:S(2)}, u32[]{:S(2)}) collective-permute-start(bf16[128,4096]{1,0:T(8,128)(2,1)S(1)} %get-tuple-element.12), channel_id=1, source_target_pairs={{1,0},{2,1},{3,2},{4,3},{5,4},{6,5},{7,6},{8,7},{9,8},{10,9},{11,1... | collective-permute-start | bytes 3145736 | tf_op jit(solution)/shard_map/ppermute | solution.py:23
  213.3 3.8 copy-start.5
  217.1 7.2 %copy-start = (bf16[256,16,1,128]{3,2,1,0:T(2,128)(2,1)}, bf16[256,16,1,128]{3,2,1,0:T(2,128)(2,1)S(1)}, u32[]{:S(2)}) copy-start(bf16[256,16,1,128]{3,2,1,0:T(2,128)(2,1)S(1)} %get-tuple-element.9) | copy-start | bytes 3145732
  217.1 7.2 %copy-start.3 = (bf16[256,16,1,128]{3,2,1,0:T(2,128)(2,1)S(1)}, bf16[256,16,1,128]{3,2,1,0:T(2,128)(2,1)}, u32[]{:S(2)}) copy-start(bf16[256,16,1,128]{3,2,1,0:T(2,128)(2,1)} %copy-done.2) | copy-start | bytes 3145732
  302.9 8.3 %copy-start.1 = (bf16[256,16,1,128]{3,2,1,0:T(2,128)(2,1)S(1)}, bf16[256,16,1,128]{3,2,1,0:T(2,128)(2,1)}, u32[]{:S(2)}) copy-start(bf16[256,16,1,128]{3,2,1,0:T(2,128)(2,1)} %copy-done) | copy-start | bytes 3145732
  311.2 93.5 %copy-start.8 = (f32[1,16,128]{2,1,0:T(8,128)S(1)}, f32[1,16,128]{2,1,0:T(8,128)}, u32[]{:S(2)}) copy-start(f32[1,16,128]{2,1,0:T(8,128)} %param.10) | copy-start | bytes 24580
  311.2 93.5 %copy-start.9 = (f32[1,16,128]{2,1,0:T(8,128)S(1)}, f32[1,16,128]{2,1,0:T(8,128)}, u32[]{:S(2)}) copy-start(f32[1,16,128]{2,1,0:T(8,128)} %param.12) | copy-start | bytes 24580
  311.2 93.5 %copy-start.10 = (f32[1,16,128]{2,1,0:T(8,128)S(1)}, f32[1,16,128]{2,1,0:T(8,128)}, u32[]{:S(2)}) copy-start(f32[1,16,128]{2,1,0:T(8,128)} %param.11) | copy-start | bytes 24580
  404.7 13.2 %collective-permute-start.17 = (f32[16,128]{1,0:T(8,128)S(1)}, f32[16,128]{1,0:T(8,128)S(1)}, u32[]{:S(2)}, u32[]{:S(2)}) collective-permute-start(f32[16,128]{1,0:T(8,128)S(1)} %fusion.17), channel_id=1, source_target_pairs={{0,16},{16,0},{1,17},{17,1},{2,18},{18,2},{3,19},{19,3},{4,20},{20... | collective-permute-start | bytes 24584 | tf_op jit(solution)/shard_map/ppermute | solution.py:17
Sparse Core Ops, SparseCore 0:
  311.3 90.2 all-reduce.3
